TPU v7x, 256 devices: a whole 4x4x8 slice. The times are simulated.
256 devices in a mesh: seq: 64 (over x, z, core), tp: 4 (over y).
Axes of the slice: x: 4, y: 4, z: 8, core: 2. Of those that a mesh axis runs over, the one named last changes fastest.
Arguments:
- hidden_states: bfloat16 [16384, 3584], P('seq', 'tp'), may hold values from -6 to 6
- queries: bfloat16 [16384, 3584], P('seq', 'tp'), may hold values from -6 to 6
- key_weight: bfloat16 [3584, 512], P(None, 'tp'), may hold values from -0.09375 to 0.09375
- value_weight: bfloat16 [3584, 512], P(None, 'tp'), may hold values from -0.09375 to 0.09375
- output_weight: bfloat16 [3584, 3584], P('tp'), may hold values from -1.5 to 1.5
- prefix_keys: bfloat16 [16384, 512], P('seq', 'tp'), may hold values from -64 to 64
- prefix_values: bfloat16 [16384, 512], P('seq', 'tp'), may hold values from -6 to 6
- reads: int32 [64, 16], replicated, may hold values from 0 to 255, as said below
- out_grad: bfloat16 [16384, 3584], P('seq', 'tp'), may hold values from -6 to 6
Outputs:
- layer_output: bfloat16 [16384, 3584], P('seq', 'tp')
- prefix_key_grad: float32 [16384, 512], P('seq', 'tp')
- prefix_value_grad: float32 [16384, 512], P('seq', 'tp')
Inputs may be any that keep to these rules, and one draw needn't show every extreme that they name: Entry l of a row is the row's node at depth l of a prefix tree, one of the blocks l * (16) to (l + 1) * 16 - 1; two rows that share a node share all its ancestors, and all rows share the root. Block b is held by index b // 4 of seq; every row names exactly 1 block of each index that it reads from.
All inputs are finite; a program needn't handle non-finite values.
Results may differ from a plain program's by a relative error of at most 0.0095.
Values may be sent and summed in bfloat16 or wider, within the bound.
A program may use at most 128 MiB of HBM per device.

v0:
```python
import jax
import jax.numpy as jnp
from jax import lax
from jax.sharding import PartitionSpec as P

QH = 28
KVH = 4
HD = 128
PBLK = 64


def local(
    hidden_states,
    queries,
    key_weight,
    value_weight,
    output_weight,
    prefix_keys,
    prefix_values,
    reads,
    out_grad,
):
    length = hidden_states.shape[0]
    scaling = HD ** (-0.5)
    groups = QH // KVH
    cache_cols = key_weight.shape[1]
    seq_count = lax.axis_size("seq")
    own_index = lax.axis_index("seq")
    blocks_here = prefix_keys.shape[0] // PBLK
    flat_width = PBLK * 2 * cache_cols
    read_count = reads.shape[1]
    hidden_piece = lax.all_gather(hidden_states, "tp", axis=1, tiled=True)
    grad_piece = lax.all_gather(out_grad, "tp", axis=1, tiled=True)
    new_keys = jnp.dot(hidden_piece, key_weight, preferred_element_type=jnp.float32)
    new_values = jnp.dot(hidden_piece, value_weight, preferred_element_type=jnp.float32)
    context_grad = lax.dot_general(
        grad_piece, output_weight, (((1,), (1,)), ((), ())), preferred_element_type=jnp.float32
    )
    new_keys = new_keys.astype(jnp.bfloat16)
    new_values = new_values.astype(jnp.bfloat16)
    context_grad = context_grad.astype(jnp.bfloat16)
    my_reads = lax.dynamic_slice_in_dim(reads, own_index, 1, 0)[0]
    local_cache = jnp.concatenate([prefix_keys, prefix_values], axis=1).reshape(
        blocks_here, flat_width
    )
    everything = lax.all_gather(local_cache, "seq", axis=0, tiled=True)
    fetched = jnp.take(everything, my_reads, axis=0)
    fetched_rows = fetched.reshape(read_count * PBLK, 2 * cache_cols)
    causal = jnp.arange(length)[None, :] <= jnp.arange(length)[:, None]
    context_parts = []
    keys_prefix = fetched_rows[:, 0:HD]
    values_prefix = fetched_rows[:, cache_cols : cache_cols + HD]
    key_total = jnp.zeros((read_count * PBLK, HD), jnp.float32)
    value_total = jnp.zeros((read_count * PBLK, HD), jnp.float32)
    for member in range(groups):
        column = member * HD
        head_queries = queries[:, column : column + HD]
        head_grads = context_grad[:, column : column + HD]
        scores_prefix = (
            jnp.einsum("td,pd->tp", head_queries, keys_prefix, preferred_element_type=jnp.float32)
            * scaling
        )
        scores_own = (
            jnp.einsum("td,ud->tu", head_queries, new_keys, preferred_element_type=jnp.float32)
            * scaling
        )
        masked_own = jnp.where(causal, scores_own, -jnp.inf)
        peak_score = jnp.maximum(jnp.max(scores_prefix, axis=-1), jnp.max(masked_own, axis=-1))[
            :, None
        ]
        exps_prefix = jnp.exp(scores_prefix - peak_score)
        exps_own = jnp.exp(masked_own - peak_score)
        denominator = (jnp.sum(exps_prefix, axis=-1) + jnp.sum(exps_own, axis=-1))[:, None]
        softmax_prefix = exps_prefix / denominator
        softmax_own = exps_own / denominator
        weights_prefix = softmax_prefix.astype(jnp.bfloat16)
        weights_own = softmax_own.astype(jnp.bfloat16)
        context = jnp.dot(weights_prefix, values_prefix, preferred_element_type=jnp.float32)
        context = context + jnp.dot(weights_own, new_values, preferred_element_type=jnp.float32)
        context_parts.append(context.astype(jnp.bfloat16))
        slope_prefix = jnp.einsum(
            "td,pd->tp", head_grads, values_prefix, preferred_element_type=jnp.float32
        )
        slope_own = jnp.einsum(
            "td,ud->tu", head_grads, new_values, preferred_element_type=jnp.float32
        )
        row_delta = jnp.sum(softmax_prefix * slope_prefix, axis=-1) + jnp.sum(
            softmax_own * slope_own, axis=-1
        )
        score_grad = (softmax_prefix * (slope_prefix - row_delta[:, None])).astype(jnp.bfloat16)
        value_total = value_total + jnp.einsum(
            "tp,td->pd", weights_prefix, head_grads, preferred_element_type=jnp.float32
        )
        key_total = key_total + jnp.einsum(
            "tp,td->pd", score_grad, head_queries, preferred_element_type=jnp.float32
        )
    key_parts = [key_total * scaling]
    value_parts = [value_total]
    attention = jnp.concatenate(context_parts, axis=1)
    cache_grads = jnp.concatenate(key_parts + value_parts, axis=1).reshape(read_count, flat_width)
    partial_value = jnp.dot(attention, output_weight, preferred_element_type=jnp.float32)
    layer_output = lax.psum_scatter(
        partial_value.astype(jnp.bfloat16), "tp", scatter_dimension=1, tiled=True
    )
    spread = (
        jnp.zeros((seq_count * blocks_here, flat_width), jnp.float32).at[my_reads].set(cache_grads)
    )
    summed = lax.psum_scatter(spread, "seq", scatter_dimension=0, tiled=True)
    summed_rows = summed.reshape(blocks_here * PBLK, 2 * cache_cols)
    return (layer_output, summed_rows[:, :cache_cols], summed_rows[:, cache_cols:])


def solution(mesh):
    in_specs = (
        P("seq", "tp"),
        P("seq", "tp"),
        P(None, "tp"),
        P(None, "tp"),
        P("tp", None),
        P("seq", "tp"),
        P("seq", "tp"),
        P(),
        P("seq", "tp"),
    )
    out_specs = (P("seq", "tp"), P("seq", "tp"), P("seq", "tp"))
    return jax.shard_map(local, mesh=mesh, in_specs=in_specs, out_specs=out_specs, check_vma=False)
```

profile of v0, /device:TPU:1, one launch (start us, length us, event | category | flops | bytes accessed | tf_op | source)
XLA Modules:
  0.0 477.5 jit_solution(8328261768748343851)
XLA Ops:
  7.2 0.7 all-gather.5.cloned.1.call-update
  8.0 0.7 all-gather.7.cloned.1.call-update
  8.7 0.9 pad_maximum_fusion.1
  9.6 0.7 reshape.176
  10.4 0.9 dynamic-slice_reduce_fusion
  11.5 33.5 %all-gather.5.cloned.1.call-done = bf16[256,3584]{1,0:T(8,128)(2,1)} async-done(((bf16[256,896]{1,0:T(8,128)(2,1)}), bf16[256,3584]{1,0:T(8,128)(2,1)}) %all-gather.5.cloned.1.call-update) | async-done | bytes 1835024 | tf_op jit(solution)/shard_map/all_gather | solution.py:32
  45.0 2.1 convolution_convert_fusion.3
  47.1 1.7 fusion.211
  48.8 1.7 fusion.213
  50.6 1.1 fusion.215
  51.6 1.1 fusion.217
  52.7 1.1 fusion.219
  54.2 2.1 convolution_convert_fusion.2
  56.3 21.7 %all-gather.7.cloned.1.call-done = bf16[256,3584]{1,0:T(8,128)(2,1)} async-done(((bf16[256,896]{1,0:T(8,128)(2,1)}), bf16[256,3584]{1,0:T(8,128)(2,1)}) %all-gather.7.cloned.1.call-update) | async-done | bytes 1835024 | tf_op jit(solution)/shard_map/all_gather | solution.py:33
  78.1 6.2 %convolution_convert_fusion.1 = bf16[256,896]{1,0:T(8,128)(2,1)} fusion(bf16[256,3584]{1,0:T(8,128)(2,1)} %all-gather.7.cloned.1.call-done, bf16[896,3584]{1,0:T(8,128)(2,1)} %param.13), kind=kOutput, calls=%fused_computation.12 | convolution fusion | flops 1644396544 | bytes 8716288 | tf_op jit(solution)/shard_map/dot_general | solution.py:36
  84.3 80.6 %all-gather.9.cloned.1.call-done = bf16[64,4,16384]{2,1,0:T(4,128)(2,1)} async-done(((bf16[1,4,16384]{2,1,0:T(4,128)(2,1)}), bf16[64,4,16384]{2,1,0:T(4,128)(2,1)}) %all-gather.9.cloned.1.call-update) | async-done | bytes 8388624 | tf_op jit(solution)/shard_map/all_gather | solution.py:46
  164.9 12.5 %reshape.177 = bf16[256,16384]{1,0:T(8,128)(2,1)} reshape(bf16[64,4,16384]{2,1,0:T(4,128)(2,1)} %all-gather.9.cloned.1.call-done) | data formatting | bytes 16777216
  177.4 5.8 %gather_fusion = bf16[16,16384]{1,0:T(8,128)(2,1)S(1)} fusion(bf16[256,16384]{1,0:T(8,128)(2,1)} %reshape.177, s32[1024]{0:T(1024)S(1)} %pad_clamp_fusion), kind=kCustom, calls=%fused_computation | custom fusion | bytes 1048640 | tf_op jit(solution)/shard_map/jit(_take)/gather | solution.py:47
  183.7 0.3 fusion.210
  184.0 0.3 fusion.212
  184.4 0.3 fusion.214
  184.8 0.3 fusion.216
  185.1 0.3 fusion.218
  185.8 0.3 fusion.222
  186.5 1.2 fusion.81
  187.7 1.4 fusion.50
  190.0 1.3 fusion.48
  192.1 1.3 fusion.46
  194.1 1.4 fusion.44
  196.2 1.3 fusion.42
  198.3 1.3 fusion.40
  200.3 1.3 fusion.38
  201.6 0.4 fusion.25
  202.0 0.4 fusion.27
  202.3 0.4 fusion.29
  202.7 0.4 fusion.31
  203.1 0.4 fusion.33
  203.5 0.4 fusion.35
  203.9 0.4 fusion.37
  204.2 1.0 slice-done
  205.3 0.8 slice-done.1
  206.1 2.3 convolution_convert_fusion
  208.4 2.3 copy.63
  210.8 1.8 convolution_add_fusion.5
  213.0 1.7 convolution_add_fusion.4
  214.7 0.4 convolution_add_fusion.3
  215.1 0.4 convolution_add_fusion.2
  215.5 0.4 convolution_add_fusion.1
  215.9 1.6 convolution_add_fusion
  217.5 0.4 fusion.66
  218.0 0.4 convolution_add_fusion.11
  218.4 0.4 convolution_add_fusion.10
  218.9 0.4 convolution_add_fusion.9
  219.3 0.4 convolution_add_fusion.8
  220.0 0.4 convolution_add_fusion.7
  220.4 0.4 fusion.2
  221.5 7.9 %scatter_custom_fusion = f32[256,16384]{1,0:T(8,128)} fusion(s32[16]{0:T(128)S(1)} %fusion.173, f32[16,16384]{1,0:T(8,128)S(1)} %reshape.172, f32[]{:T(128)} %constant.9.clone.1), kind=kCustom, calls=%fused_computation.2 | custom fusion | bytes 16777220 | tf_op jit(solution)/shard_map/scatter | solution.py:106
  229.4 0.7 copy-done.20
  230.2 0.6 dynamic-slice
  231.4 6.6 %reduce-scatter.4.cloned.1.call-done = bf16[896,256]{1,0:T(8,128)(2,1)} async-done(((bf16[3584,256]{1,0:T(8,128)(2,1)}), bf16[896,256]{1,0:T(8,128)(2,1)}) %reduce-scatter.4.cloned.1.call-update) | async-done | bytes 458768
  238.0 2.0 copy.64
  240.0 229.0 %all-reduce.3.cloned.1.call-done = f32[256,16384]{1,0:T(8,128)} async-done(((f32[256,16384]{1,0:T(8,128)}), f32[256,16384]{1,0:T(8,128)}) %all-reduce.3.cloned.1.call-update) | async-done | bytes 16777232
  468.9 1.1 constant_dynamic-slice_fusion
  470.2 0.7 fusion.209
  (133 shorter events, 8.2 us)
Async XLA Ops:
  7.2 37.8 %copy-start = (bf16[3584,128]{1,0:T(8,128)(2,1)S(1)}, bf16[3584,128]{1,0:T(8,128)(2,1)}, u32[]{:S(2)}) copy-start(bf16[3584,128]{1,0:T(8,128)(2,1)} %param.11) | copy-start | bytes 2752516
  7.2 46.6 %copy-start.17 = (bf16[256,896]{1,0:T(8,128)(2,1)S(1)}, bf16[256,896]{1,0:T(8,128)(2,1)}, u32[]{:S(2)}) copy-start(bf16[256,896]{1,0:T(8,128)(2,1)} %param.10) | copy-start | bytes 1376260
  7.2 47.0 %copy-start.16 = (bf16[3584,128]{1,0:T(8,128)(2,1)S(1)}, bf16[3584,128]{1,0:T(8,128)(2,1)}, u32[]{:S(2)}) copy-start(bf16[3584,128]{1,0:T(8,128)(2,1)} %param.12) | copy-start | bytes 2752516
  7.2 37.8 %all-gather.5.cloned.1.call-start = ((), (), s32[]{:S(2)}) async-start(), calls=%async_computation.1 | async-start | bytes 2293760 | tf_op jit(solution)/shard_map/all_gather | solution.py:32
  7.9 70.1 %all-gather.7.cloned.1.call-start = ((), (), s32[]{:S(2)}) async-start(), calls=%async_computation.2 | async-start | bytes 2293760 | tf_op jit(solution)/shard_map/all_gather | solution.py:33
  8.7 156.2 %all-gather.9.cloned.1.call-start = ((), (), s32[]{:S(2)}) async-start(), calls=%async_computation.3 | async-start | bytes 8519680 | tf_op jit(solution)/shard_map/all_gather | solution.py:46
  10.4 227.6 %reduce-scatter.4.cloned.1.call-start = ((), (), s32[]{:S(2)}) async-start(), calls=%async_computation.4 | async-start | bytes 2293760
  183.2 3.2 copy-start.19
  183.5 3.1 copy-start.21
  184.0 17.6 %copy-start.14 = (f32[1024,256]{1,0:T(8,128)}, f32[1024,256]{1,0:T(8,128)S(1)}, u32[]{:S(2)}) copy-start(f32[1024,256]{1,0:T(8,128)S(1)} %get-tuple-element.6) | copy-start | bytes 3145732
  184.4 17.6 %copy-start.12 = (f32[1024,256]{1,0:T(8,128)}, f32[1024,256]{1,0:T(8,128)S(1)}, u32[]{:S(2)}) copy-start(f32[1024,256]{1,0:T(8,128)S(1)} %get-tuple-element.10) | copy-start | bytes 3145732
  184.7 17.6 %copy-start.10 = (f32[1024,256]{1,0:T(8,128)}, f32[1024,256]{1,0:T(8,128)S(1)}, u32[]{:S(2)}) copy-start(f32[1024,256]{1,0:T(8,128)S(1)} %get-tuple-element.14) | copy-start | bytes 3145732
  185.1 17.6 %copy-start.8 = (f32[1024,256]{1,0:T(8,128)}, f32[1024,256]{1,0:T(8,128)S(1)}, u32[]{:S(2)}) copy-start(f32[1024,256]{1,0:T(8,128)S(1)} %get-tuple-element.18) | copy-start | bytes 3145732
  185.5 17.6 %copy-start.6 = (f32[1024,256]{1,0:T(8,128)}, f32[1024,256]{1,0:T(8,128)S(1)}, u32[]{:S(2)}) copy-start(f32[1024,256]{1,0:T(8,128)S(1)} %get-tuple-element.22) | copy-start | bytes 3145732
  185.8 17.7 %copy-start.4 = (f32[1024,256]{1,0:T(8,128)}, f32[1024,256]{1,0:T(8,128)S(1)}, u32[]{:S(2)}) copy-start(f32[1024,256]{1,0:T(8,128)S(1)} %get-tuple-element.26) | copy-start | bytes 3145732
  186.2 17.7 %copy-start.2 = (f32[1024,256]{1,0:T(8,128)}, f32[1024,256]{1,0:T(8,128)S(1)}, u32[]{:S(2)}) copy-start(f32[1024,256]{1,0:T(8,128)S(1)} %get-tuple-element.30) | copy-start | bytes 3145732
  186.4 3.3 copy-start.18
  203.1 2.2 slice-start
  203.5 2.6 slice-start.1
  206.1 4.7 copy-start.22
  210.7 3.9 copy-start.9
  210.8 4.3 copy-start.7
  210.8 258.2 %all-reduce.3.cloned.1.call-start = ((), (), s32[]{:S(2)}) async-start(), calls=%async_computation.5 | async-start | bytes 33554432
  213.0 2.5 copy-start.5
  214.7 1.2 copy-start.3
  215.1 2.5 copy-start.15
  215.1 2.5 copy-start.29
  215.5 2.5 copy-start.13
  215.5 2.5 copy-start.23
  215.9 2.5 copy-start.11
  215.9 2.5 copy-start.24
  217.5 1.4 copy-start.25
  218.0 1.3 copy-start.26
  218.4 1.6 copy-start.27
  218.9 1.5 copy-start.28
  229.4 241.5 %copy-start.1 = (bf16[3584,128]{1,0:T(8,128)(2,1)S(1)}, bf16[3584,128]{1,0:T(8,128)(2,1)}, u32[]{:S(2)}) copy-start(bf16[3584,128]{1,0:T(8,128)(2,1)} %param.11) | copy-start | bytes 2752516
  229.4 0.8 copy-start.20
Sparse Core Ops, SparseCore 0:
  9.9 35.0 all-gather.4
  46.8 31.2 all-gather.6
  81.4 83.3 all-gather.8
  210.9 27.0 reduce-scatter.3
  241.5 227.3 all-reduce.2
where the time goes:
time: 478 us; the launch traced here: 477 us
  waiting for transfers between devices  373 us (78%)
  matrix products  47.3 us (10%)
  local copies, waits for them, and re-layouts  38.8 us (8%)
  between operations  15.2 us (3%)
    unnamed x7, waiting for transfers between devices  237 us
    all_gather x1, waiting for transfers between devices, local(): everything = lax.all_gather(local_cache, 'seq', axis=0, tiled=True)  80.6 us
    all_gather x1, waiting for transfers between devices, local(): hidden_piece = lax.all_gather(hidden_states, 'tp', axis=1, tiled=True)  33.5 us
    unnamed x70, local copies, waits for them, and re-layouts  22.3 us
    all_gather x1, waiting for transfers between devices, local(): grad_piece = lax.all_gather(out_grad, 'tp', axis=1, tiled=True)  21.7 us
  transfers between devices with their start and end apart: 5, of which 5 were waited for; matrix products, arithmetic and copies ran while one was open for 9% of the time, Pallas kernels for 0%

commit v1 on v0

v1 whole, which is shorter than its diff:
```python
import functools

import jax
import jax.numpy as jnp
from jax import lax
from jax.experimental import pallas as pl
from jax.experimental.pallas import tpu as pltpu
from jax.sharding import PartitionSpec as P

HD = 128
PBLK = 64
NX, NZ = 4, 8
TP = 4
HEADS = 7
TOK = 256
KEYS = 1024
ALL = KEYS + TOK
FEAT = 896
HALF = TOK // 2
SCALE = HD ** -0.5
LOG2E = 1.4426950408889634
BF = jnp.bfloat16
F32 = jnp.float32
MESH = pl.DeviceIdType.MESH


def dot(a, b):
    return jnp.dot(a, b, preferred_element_type=F32)


def dot_nt(a, b):
    return lax.dot_general(a, b, (((1,), (1,)), ((), ())), preferred_element_type=F32)


def kernel(
    reads, hid, queries, key_w, value_w, out_w, pkeys, pvalues, og,
    out, gk, gv,
    hs, gs, wkv, wo, qv, qt, grp, snd, kv, vt, hot, st, es, ctxt, ctx, inv, cgacc, cgt, cgn,
    dss, gsend, grecv, psend, precv, own_grad, rs_own, rs_fwd, rs_mid, rs_in,
    load_sem, ys_sem, yr_sem, g_send, g_recv, a_send, a_recv, b_send, b_recv, p_send, p_recv,
    r_send, r_recv,
):
    seq = lax.axis_index("seq")
    tp = lax.axis_index("tp")
    core = seq % 2
    zpos = (seq // 2) % NZ
    xpos = seq // (2 * NZ)
    member = seq % 4
    level = seq // 4
    right = (tp + 1) % TP
    left = (tp + TP - 1) % TP
    across = (tp + 2) % TP
    step = 2 * (zpos % 2) - 1

    def seq_of(x, z):
        return (x * NZ + z) * 2 + core

    def reader(r):
        i, j = r // 4, r % 4
        return seq_of((xpos + i) % NX, (zpos + step * j + NZ) % NZ)

    def server(r):
        i, j = r // 4, r % 4
        even = (zpos + j) % 2
        z = (zpos + j - 2 * j * even + NZ) % NZ
        return seq_of((xpos + NX - i) % NX, z)

    def peer(p):
        low = member
        bit0, bit1 = low % 2, low // 2
        if p % 2:
            bit0 = 1 - bit0
        if p // 2:
            bit1 = 1 - bit1
        return bit1 * 2 + bit0

    barrier = pltpu.get_barrier_semaphore()
    for t in (left, right):
        pl.semaphore_signal(barrier, 1, device_id={"tp": t}, device_id_type=MESH)
    for p in (1, 2, 3):
        pl.semaphore_signal(
            barrier, 1, device_id={"seq": level * 4 + peer(p)}, device_id_type=MESH
        )
    for r in range(1, 16):
        pl.semaphore_signal(barrier, 1, device_id={"seq": reader(r)}, device_id_type=MESH)
        pl.semaphore_signal(barrier, 1, device_id={"seq": server(r)}, device_id_type=MESH)

    loads = []

    def load(src, dst):
        loads.append(pltpu.make_async_copy(src, dst, load_sem.at[len(loads)]))
        loads[-1].start()

    load(hid, hs.at[3])
    load(queries, qv)
    for j in range(TP):
        load(key_w.at[pl.ds(j * FEAT, FEAT)], wkv.at[j, :, pl.ds(0, HD)])
        load(value_w.at[pl.ds(j * FEAT, FEAT)], wkv.at[j, :, pl.ds(HD, HD)])
    load(og, gs.at[3])
    for j in range(TP):
        load(out_w.at[:, pl.ds(j * FEAT, FEAT)], wo.at[j])

    for b in range(4):
        grp[member * 4 + b, :, 0:HD] = pkeys[b * PBLK : (b + 1) * PBLK, :]
        grp[member * 4 + b, :, HD:] = pvalues[b * PBLK : (b + 1) * PBLK, :]

    pl.semaphore_wait(barrier, 35)

    def ring(src, dst, k):
        lo, hi = pl.ds(0, HALF), pl.ds(HALF, HALF)

        def copy(s, d, n, to):
            return pltpu.make_async_remote_copy(
                s, d, ys_sem.at[k + n], yr_sem.at[k + n],
                device_id={"tp": to}, device_id_type=MESH,
            )

        own = [
            copy(src.at[lo], dst.at[0, lo], 0, right),
            copy(src.at[hi], dst.at[1, hi], 1, left),
            copy(src.at[hi], dst.at[0, hi], 2, right),
            copy(src.at[lo], dst.at[1, lo], 3, left),
        ]
        forward = [
            copy(dst.at[0, lo], dst.at[2, lo], 4, right),
            copy(dst.at[1, hi], dst.at[2, hi], 5, left),
        ]
        return own, forward

    h_own, h_fwd = ring(hid, hs, 0)
    o_own, o_fwd = ring(og, gs, 6)
    for c in h_own:
        c.start()

    group = []
    for p in (3, 2, 1):
        c = pltpu.make_async_remote_copy(
            grp.at[pl.ds(member * 4, 4)], grp.at[pl.ds(member * 4, 4)],
            g_send.at[p], g_recv.at[p],
            device_id={"seq": level * 4 + peer(p)}, device_id_type=MESH,
        )
        c.start()
        group.append(c)

    rd = [lax.bitwise_and(reads[reader(r), level], 15) for r in range(16)]
    lane = lax.broadcasted_iota(jnp.int32, (TOK, 128), 1)
    sub = lax.broadcasted_iota(jnp.int32, (TOK, 128), 0)
    for h in range(8):
        want = jnp.where(lane < PBLK, rd[2 * h] * PBLK + lane, rd[2 * h + 1] * PBLK + lane - PBLK)
        for p in range(4):
            match = (sub + peer(p) * TOK) == want
            hot[p, :, h * 128 : (h + 1) * 128] = jnp.where(match, 1.0, 0.0).astype(BF)

    loads[1].wait()
    for h in range(HEADS):
        qt[h] = qv[:, h * HD : (h + 1) * HD].T

    h_own[0].wait_recv()
    h_fwd[0].start()
    h_own[1].wait_recv()
    h_fwd[1].start()

    for c in group:
        c.wait_recv()
    serve = [None]
    kv[0:PBLK, :] = grp[rd[0]]
    for r in range(1, 16):
        snd[r] = grp[rd[r]]
        c = pltpu.make_async_remote_copy(
            snd.at[r], kv.at[pl.ds(r * PBLK, PBLK)], a_send.at[r], a_recv.at[r],
            device_id={"seq": reader(r)}, device_id_type=MESH,
        )
        c.start()
        serve.append(c)

    loads[0].wait()
    for n in range(2, 10):
        loads[n].wait()
    total = dot(hs[3], wkv[tp])
    h_own[2].wait_recv()
    total += dot(hs[0], wkv[left])
    h_own[3].wait_recv()
    total += dot(hs[1], wkv[right])
    for c in o_own:
        c.start()
    h_fwd[0].wait_recv()
    h_fwd[1].wait_recv()
    total += dot(hs[2], wkv[across])
    kv[KEYS:ALL, :] = total.astype(BF)

    for r in range(1, 16):
        serve[r].wait_recv()
    vt[...] = kv[:, HD:].T

    key_pos = lax.broadcasted_iota(jnp.int32, (TOK, TOK), 0)
    tok_pos = lax.broadcasted_iota(jnp.int32, (TOK, TOK), 1)

    def forward(h, _):
        q_h = qt[h]
        peak = None
        for c in range(5):
            s = dot(kv[c * TOK : (c + 1) * TOK, 0:HD], q_h)
            if c == 4:
                s = jnp.where(key_pos <= tok_pos, s, -jnp.inf)
            st[c] = s
            top = jnp.max(s, axis=0, keepdims=True)
            peak = top if peak is None else jnp.maximum(peak, top)
        low = None
        for c in range(5):
            e = jnp.exp2((st[c] - peak) * (SCALE * LOG2E))
            part = jnp.sum(e, axis=0, keepdims=True)
            low = part if low is None else low + part
            es[h, c * TOK : (c + 1) * TOK, :] = e.astype(BF)
        scale = 1.0 / low
        inv[h] = jnp.broadcast_to(scale, (8, TOK))
        ctxt[h] = dot(vt[...], es[h]) * scale
        return 0

    lax.fori_loop(0, 4, forward, 0)
    o_own[0].wait_recv()
    o_fwd[0].start()
    o_own[1].wait_recv()
    o_fwd[1].start()
    lax.fori_loop(4, HEADS, forward, 0)
    for h in range(HEADS):
        ctx[:, h * HD : (h + 1) * HD] = ctxt[h].astype(BF).T

    for n in range(11, 15):
        loads[n].wait()

    def rs(src, dst, n, to):
        return pltpu.make_async_remote_copy(
            src, dst, r_send.at[n], r_recv.at[n], device_id={"tp": to}, device_id_type=MESH
        )

    lo, hi = pl.ds(0, HALF), pl.ds(HALF, HALF)
    rs_far = [
        rs(rs_fwd.at[lo], rs_mid.at[0], 0, right),
        rs(rs_fwd.at[hi], rs_mid.at[1], 1, left),
    ]
    rs_now = [
        rs(rs_own.at[0, hi], rs_in.at[0, hi], 2, right),
        rs(rs_own.at[1, lo], rs_in.at[1, lo], 3, left),
    ]
    rs_late = [
        rs(rs_own.at[0, lo], rs_in.at[0, lo], 4, right),
        rs(rs_own.at[1, hi], rs_in.at[1, hi], 5, left),
    ]
    rs_fwd[...] = dot(ctx[...], wo[across]).astype(BF)
    for c in rs_far:
        c.start()
    rs_own[0] = dot(ctx[...], wo[right]).astype(BF)
    rs_own[1] = dot(ctx[...], wo[left]).astype(BF)
    for c in rs_now:
        c.start()

    loads[10].wait()
    cgacc[...] = dot_nt(wo[tp], gs[3])
    o_own[2].wait_recv()
    cgacc[...] += dot_nt(wo[left], gs[0])
    o_own[3].wait_recv()
    cgacc[...] += dot_nt(wo[right], gs[1])
    o_fwd[0].wait_recv()
    o_fwd[1].wait_recv()
    cgacc[...] += dot_nt(wo[across], gs[2])
    for h in range(HEADS):
        scaled = (cgacc[h * HD : (h + 1) * HD, :] * inv[h, 0:1, :]).astype(BF)
        cgt[h] = scaled
        cgn[h] = scaled.T
        delta = jnp.sum(scaled.astype(F32) * ctxt[h], axis=0, keepdims=True)
        inv[h] = jnp.broadcast_to(delta, (8, TOK))

    back = [None] * 16

    def backward(i):
        rows = slice(i * TOK, (i + 1) * TOK)
        vals = kv[rows, HD:]
        dk = None
        for h in range(HEADS):
            slope = dot(vals, cgt[h])
            e = es[h, rows, :]
            grad = (e.astype(F32) * (slope - inv[h, 0:1, :])).astype(BF)
            dk_h = dot(grad, qv[:, h * HD : (h + 1) * HD])
            dv_h = dot(e, cgn[h])
            dk = dk_h if dk is None else dk + dk_h
            dv = dv_h if h == 0 else dv + dv_h
        gsend[rows, 0:HD] = dk.astype(BF)
        gsend[rows, HD:] = dv.astype(BF)
        for j in range(4):
            r = i * 4 + j
            if r == 0:
                grecv[0:PBLK, :] = gsend[0:PBLK, :]
                continue
            place = pl.ds(r * PBLK, PBLK)
            c = pltpu.make_async_remote_copy(
                gsend.at[place], grecv.at[place], b_send.at[r], b_recv.at[r],
                device_id={"seq": server(r)}, device_id_type=MESH,
            )
            c.start()
            back[r] = c

    backward(2)
    backward(1)
    rs_far[0].wait_recv()
    rs_own[0, 0:HALF] = (rs_own[0, 0:HALF].astype(F32) + rs_mid[0].astype(F32)).astype(BF)
    rs_late[0].start()
    rs_far[1].wait_recv()
    rs_own[1, HALF:] = (rs_own[1, HALF:].astype(F32) + rs_mid[1].astype(F32)).astype(BF)
    rs_late[1].start()
    backward(3)
    backward(0)

    mine = dot(ctx[...], wo[tp])

    for r in range(1, 16):
        back[r].wait_recv()
    spread = []
    for p in (3, 2, 1):
        psend[p] = dot(hot[p], grecv[...]).astype(BF)
        c = pltpu.make_async_remote_copy(
            psend.at[p], precv.at[p], p_send.at[p], p_recv.at[p],
            device_id={"seq": level * 4 + peer(p)}, device_id_type=MESH,
        )
        c.start()
        spread.append(c)
    own_grad[...] = dot(hot[0], grecv[...])

    for c in rs_now + rs_late:
        c.wait_recv()
    out[...] = (mine + rs_in[0].astype(F32) + rs_in[1].astype(F32)).astype(BF)

    for c in spread:
        c.wait_recv()
    total = own_grad[...] + precv[1].astype(F32) + precv[2].astype(F32) + precv[3].astype(F32)
    gk[...] = total[:, 0:HD] * SCALE
    gv[...] = total[:, HD:]

    for c in h_own + h_fwd + o_own + o_fwd + group + rs_far + rs_now + rs_late + spread:
        c.wait_send()
    for r in range(1, 16):
        serve[r].wait_send()
        back[r].wait_send()


def local(*args):
    hidden, queries, key_w, value_w, out_w, pkeys, pvalues, reads, og = args
    vmem = pl.BlockSpec(memory_space=pltpu.VMEM)
    hbm = pl.BlockSpec(memory_space=pl.ANY)
    dma = pltpu.SemaphoreType.DMA
    V = pltpu.VMEM
    return pl.pallas_call(
        kernel,
        out_shape=(
            jax.ShapeDtypeStruct((TOK, FEAT), BF),
            jax.ShapeDtypeStruct((TOK, HD), F32),
            jax.ShapeDtypeStruct((TOK, HD), F32),
        ),
        in_specs=[pl.BlockSpec(memory_space=pltpu.SMEM), hbm, hbm, hbm, hbm, hbm, vmem, vmem, hbm],
        out_specs=(vmem, vmem, vmem),
        scratch_shapes=[
            V((4, TOK, FEAT), BF),
            V((4, TOK, FEAT), BF),
            V((TP, FEAT, 2 * HD), BF),
            V((TP, FEAT, FEAT), BF),
            V((TOK, FEAT), BF),
            V((HEADS, HD, TOK), BF),
            V((16, PBLK, 2 * HD), BF),
            V((16, PBLK, 2 * HD), BF),
            V((ALL, 2 * HD), BF),
            V((HD, ALL), BF),
            V((4, TOK, KEYS), BF),
            V((5, TOK, TOK), F32),
            V((HEADS, ALL, TOK), BF),
            V((HEADS, HD, TOK), F32),
            V((TOK, FEAT), BF),
            V((HEADS, 8, TOK), F32),
            V((FEAT, TOK), F32),
            V((HEADS, HD, TOK), BF),
            V((HEADS, TOK, HD), BF),
            V((8, 128), F32),
            V((KEYS, 2 * HD), BF),
            V((KEYS, 2 * HD), BF),
            V((4, TOK, 2 * HD), BF),
            V((4, TOK, 2 * HD), BF),
            V((TOK, 2 * HD), F32),
            V((2, TOK, FEAT), BF),
            V((TOK, FEAT), BF),
            V((2, HALF, FEAT), BF),
            V((2, TOK, FEAT), BF),
            dma((15,)), dma((12,)), dma((12,)), dma((4,)), dma((4,)), dma((16,)), dma((16,)),
            dma((16,)), dma((16,)), dma((4,)), dma((4,)), dma((6,)), dma((6,)),
        ],
        compiler_params=pltpu.CompilerParams(
            collective_id=0, has_side_effects=True, vmem_limit_bytes=56 * 1024 * 1024
        ),
    )(reads, hidden, queries, key_w, value_w, out_w, pkeys, pvalues, og)


def solution(mesh):
    in_specs = (
        P("seq", "tp"), P("seq", "tp"), P(None, "tp"), P(None, "tp"), P("tp", None),
        P("seq", "tp"), P("seq", "tp"), P(), P("seq", "tp"),
    )
    out_specs = (P("seq", "tp"), P("seq", "tp"), P("seq", "tp"))
    return jax.shard_map(local, mesh=mesh, in_specs=in_specs, out_specs=out_specs, check_vma=False)
```

time: 478 us -> 74.8 us (0.16)
  waiting for transfers between devices: 373 us -> 0 us
  Pallas kernels: 0 us -> 67.5 us
  matrix products: 47.3 us -> 0 us
  local copies, waits for them, and re-layouts: 38.8 us -> 6.35 us
  between operations: 15.2 us -> 0.64 us
    unnamed x7 -> x0, waiting for transfers between devices: 237 us -> none
    all_gather x3 -> x0, waiting for transfers between devices: 136 us -> none  [the longest x1 80.6 us: local(): everything = lax.all_gather(local_cache, 'seq', axis=0, tiled=True)]
    pallas_call x0 -> x1, Pallas kernels: none -> 67.5 us  [local(): pl.pallas_call(kernel, out_shape=(jax.ShapeDtypeStruct((TOK, FEAT), BF),...]
    dot_general x60 -> x0, matrix products: 47.3 us -> none  [the longest x7 9.15 us: local(): jnp.einsum('td,pd->tp', head_grads, values_prefix, preferred_element_type...]
    unnamed x70 -> x4, local copies, waits for them, and re-layouts: 22.3 us -> 6.35 us
    scatter x1 -> x0, local copies, waits for them, and re-layouts: 7.92 us -> none  [local(): jnp.zeros((seq_count * blocks_here, flat_width), jnp.float32).at[my_reads]]
    gather x2 -> x0, local copies, waits for them, and re-layouts: 6.03 us -> none  [local(): fetched = jnp.take(everything, my_reads, axis=0)]
  transfers between devices with their start and end apart: 5 -> 0, of which waited for: 5 -> 0; matrix products, arithmetic and copies ran while one was open for 9% -> 0% of each run, Pallas kernels for 0% -> 0%
where the time goes in v1:
time: 74.8 us; the launch traced here: 74.5 us
  Pallas kernels  67.5 us (90%)
  local copies, waits for them, and re-layouts  6.35 us (8%)
    pallas_call x1, Pallas kernels, local(): pl.pallas_call(kernel, out_shape=(jax.ShapeDtypeStruct((TOK, FEAT), BF),...  67.5 us
    unnamed x4, local copies, waits for them, and re-layouts  6.35 us

profile of v1, /device:TPU:1, one launch (start us, length us, event | category | flops | bytes accessed | tf_op | source)
XLA Modules:
  0.0 74.5 jit_solution(4387074736027149780)
XLA Ops:
  0.6 1.4 %copy.12.reads = s32[64,16]{1,0:T(8,128)} copy(s32[64,16]{0,1:T(8,128)} %param.16) | data formatting | bytes 8192 | tf_op args[7]
  2.0 67.5 %shard_map.112 = (bf16[256,896]{1,0:T(8,128)(2,1)}, f32[256,128]{1,0:T(8,128)}, f32[256,128]{1,0:T(8,128)}) custom-call(s32[64,16]{1,0:T(8,128)} %copy.12.reads, bf16[256,896]{1,0:T(8,128)(2,1)} %hid.1, bf16[256,896]{1,0:T(8,128)(2,1)} %queries.1, bf16[3584,128]{1,0:T(8,128)(2,1)} %key_w.1, bf16[3584,128]{1,0:T(8,128)(2,1)} %value_w.1, ...), custom_call_target="tpu_custom_call" | custom-call | tf_op jit(solution)/shard_map/pallas_call | solution.py:351
  69.5 1.8 %copy.16 = bf16[256,896]{1,0:T(8,128)(2,1)} copy(bf16[256,896]{1,0:T(8,128)(2,1)} %get-tuple-element.6) | data formatting | bytes 917504
  71.3 1.6 %copy.17 = f32[256,128]{1,0:T(8,128)} copy(f32[256,128]{1,0:T(8,128)} %get-tuple-element.7) | data formatting | bytes 262144
  72.9 1.6 %copy.18 = f32[256,128]{1,0:T(8,128)} copy(f32[256,128]{1,0:T(8,128)} %get-tuple-element.8) | data formatting | bytes 262144

commit v2 on v1

--- a/solution.py
+++ b/solution.py
@@ -33,10 +33,10 @@
 
 
 def kernel(
-    reads, hid, queries, key_w, value_w, out_w, pkeys, pvalues, og,
-    out, gk, gv,
-    hs, gs, wkv, wo, qv, qt, grp, snd, kv, vt, hot, st, es, ctxt, ctx, inv, cgacc, cgt, cgn,
-    dss, gsend, grecv, psend, precv, own_grad, rs_own, rs_fwd, rs_mid, rs_in,
+    reads_hbm, hid, queries, key_w, value_w, out_w, pkeys, pvalues, og,
+    out, grads,
+    reads, hs, gs, wkv, wo, qv, qt, grp, snd, kv, vt, hot, st, es, ctxt, ctx, inv, cgacc, cgt, cgn,
+    gsend, grecv, psend, precv, own_grad, rs_own, rs_fwd, rs_mid, rs_in,
     load_sem, ys_sem, yr_sem, g_send, g_recv, a_send, a_recv, b_send, b_recv, p_send, p_recv,
     r_send, r_recv,
 ):
@@ -82,7 +82,6 @@
             barrier, 1, device_id={"seq": level * 4 + peer(p)}, device_id_type=MESH
         )
     for r in range(1, 16):
-        pl.semaphore_signal(barrier, 1, device_id={"seq": reader(r)}, device_id_type=MESH)
         pl.semaphore_signal(barrier, 1, device_id={"seq": server(r)}, device_id_type=MESH)
 
     loads = []
@@ -91,6 +90,19 @@
         loads.append(pltpu.make_async_copy(src, dst, load_sem.at[len(loads)]))
         loads[-1].start()
 
+    mine = grp.at[pl.ds(member * 4, 4)]
+    first = [pltpu.make_async_copy(reads_hbm, reads, load_sem.at[23])]
+    for b in range(4):
+        rows = pl.ds(b * PBLK, PBLK)
+        for n, (src, col) in enumerate(((pkeys, 0), (pvalues, HD))):
+            first.append(
+                pltpu.make_async_copy(
+                    src.at[rows], grp.at[member * 4 + b, :, pl.ds(col, HD)],
+                    load_sem.at[15 + 2 * b + n],
+                )
+            )
+    for c in first:
+        c.start()
     load(hid, hs.at[3])
     load(queries, qv)
     for j in range(TP):
@@ -100,11 +112,10 @@
     for j in range(TP):
         load(out_w.at[:, pl.ds(j * FEAT, FEAT)], wo.at[j])
 
-    for b in range(4):
-        grp[member * 4 + b, :, 0:HD] = pkeys[b * PBLK : (b + 1) * PBLK, :]
-        grp[member * 4 + b, :, HD:] = pvalues[b * PBLK : (b + 1) * PBLK, :]
-
-    pl.semaphore_wait(barrier, 35)
+    for c in first:
+        c.wait()
+
+    pl.semaphore_wait(barrier, 20)
 
     def ring(src, dst, k):
         lo, hi = pl.ds(0, HALF), pl.ds(HALF, HALF)
@@ -135,14 +146,14 @@
     group = []
     for p in (3, 2, 1):
         c = pltpu.make_async_remote_copy(
-            grp.at[pl.ds(member * 4, 4)], grp.at[pl.ds(member * 4, 4)],
+            mine, mine,
             g_send.at[p], g_recv.at[p],
             device_id={"seq": level * 4 + peer(p)}, device_id_type=MESH,
         )
         c.start()
         group.append(c)
 
-    rd = [lax.bitwise_and(reads[reader(r), level], 15) for r in range(16)]
+    rd = [lax.bitwise_and(reads[level, reader(r)], 15) for r in range(16)]
     lane = lax.broadcasted_iota(jnp.int32, (TOK, 128), 1)
     sub = lax.broadcasted_iota(jnp.int32, (TOK, 128), 0)
     for h in range(8):
@@ -310,7 +321,7 @@
     backward(3)
     backward(0)
 
-    mine = dot(ctx[...], wo[tp])
+    kept = dot(ctx[...], wo[tp])
 
     for r in range(1, 16):
         back[r].wait_recv()
@@ -327,13 +338,13 @@
 
     for c in rs_now + rs_late:
         c.wait_recv()
-    out[...] = (mine + rs_in[0].astype(F32) + rs_in[1].astype(F32)).astype(BF)
+    out[...] = (kept + rs_in[0].astype(F32) + rs_in[1].astype(F32)).astype(BF)
 
     for c in spread:
         c.wait_recv()
     total = own_grad[...] + precv[1].astype(F32) + precv[2].astype(F32) + precv[3].astype(F32)
-    gk[...] = total[:, 0:HD] * SCALE
-    gv[...] = total[:, HD:]
+    grads[:, 0:HD] = total[:, 0:HD] * SCALE
+    grads[:, HD:] = total[:, HD:]
 
     for c in h_own + h_fwd + o_own + o_fwd + group + rs_far + rs_now + rs_late + spread:
         c.wait_send()
@@ -344,20 +355,22 @@
 
 def local(*args):
     hidden, queries, key_w, value_w, out_w, pkeys, pvalues, reads, og = args
+    operands = (reads.T, hidden, queries, key_w, value_w, out_w, pkeys, pvalues, og)
+    operands = [pltpu.with_memory_space_constraint(a, pltpu.HBM) for a in operands]
     vmem = pl.BlockSpec(memory_space=pltpu.VMEM)
-    hbm = pl.BlockSpec(memory_space=pl.ANY)
+    hbm = pl.BlockSpec(memory_space=pltpu.HBM)
     dma = pltpu.SemaphoreType.DMA
     V = pltpu.VMEM
-    return pl.pallas_call(
+    out, grads = pl.pallas_call(
         kernel,
         out_shape=(
             jax.ShapeDtypeStruct((TOK, FEAT), BF),
-            jax.ShapeDtypeStruct((TOK, HD), F32),
-            jax.ShapeDtypeStruct((TOK, HD), F32),
+            jax.ShapeDtypeStruct((TOK, 2 * HD), F32),
         ),
-        in_specs=[pl.BlockSpec(memory_space=pltpu.SMEM), hbm, hbm, hbm, hbm, hbm, vmem, vmem, hbm],
-        out_specs=(vmem, vmem, vmem),
+        in_specs=[hbm] * 9,
+        out_specs=(vmem, vmem),
         scratch_shapes=[
+            pltpu.SMEM((16, 64), jnp.int32),
             V((4, TOK, FEAT), BF),
             V((4, TOK, FEAT), BF),
             V((TP, FEAT, 2 * HD), BF),
@@ -377,7 +390,6 @@
             V((FEAT, TOK), F32),
             V((HEADS, HD, TOK), BF),
             V((HEADS, TOK, HD), BF),
-            V((8, 128), F32),
             V((KEYS, 2 * HD), BF),
             V((KEYS, 2 * HD), BF),
             V((4, TOK, 2 * HD), BF),
@@ -387,13 +399,14 @@
             V((TOK, FEAT), BF),
             V((2, HALF, FEAT), BF),
             V((2, TOK, FEAT), BF),
-            dma((15,)), dma((12,)), dma((12,)), dma((4,)), dma((4,)), dma((16,)), dma((16,)),
+            dma((24,)), dma((12,)), dma((12,)), dma((4,)), dma((4,)), dma((16,)), dma((16,)),
             dma((16,)), dma((16,)), dma((4,)), dma((4,)), dma((6,)), dma((6,)),
         ],
         compiler_params=pltpu.CompilerParams(
-            collective_id=0, has_side_effects=True, vmem_limit_bytes=56 * 1024 * 1024
+            collective_id=0, has_side_effects=True, vmem_limit_bytes=40 * 1024 * 1024
         ),
-    )(reads, hidden, queries, key_w, value_w, out_w, pkeys, pvalues, og)
+    )(*operands)
+    return out, grads[:, 0:HD], grads[:, HD:]
 
 
 def solution(mesh):

time: 74.8 us -> 68.4 us (0.914)
  local copies, waits for them, and re-layouts: 6.35 us -> 1.48 us
  Pallas kernels: 67.5 us -> 66.2 us
    unnamed x4 -> x1, local copies, waits for them, and re-layouts: 6.35 us -> 0.77 us
    pallas_call x1, Pallas kernels: 67.5 us -> 66.2 us  [local(): pl.pallas_call(kernel, out_shape=(jax.ShapeDtypeStruct((TOK, FEAT), BF),...]
where the time goes in v2:
time: 68.4 us; the launch traced here: 68.3 us
  Pallas kernels  66.2 us (97%)
  local copies, waits for them, and re-layouts  1.48 us (2%)
    pallas_call x1, Pallas kernels, local(): pl.pallas_call(kernel, out_shape=(jax.ShapeDtypeStruct((TOK, FEAT), BF),...  66.2 us

profile of v2, /device:TPU:1, one launch (start us, length us, event | category | flops | bytes accessed | tf_op | source)
XLA Modules:
  0.0 68.3 jit_solution(11513510659783967692)
XLA Ops:
  0.6 66.2 %shard_map.112 = (bf16[256,896]{1,0:T(8,128)(2,1)S(1)}, f32[256,256]{1,0:T(8,128)S(1)}) custom-call(s32[16,64]{1,0:T(8,128)} %bitcast.1, bf16[256,896]{1,0:T(8,128)(2,1)} %hid.1, bf16[256,896]{1,0:T(8,128)(2,1)} %queries.1, bf16[3584,128]{1,0:T(8,128)(2,1)} %key_w.1, bf16[3584,128]{1,0:T(8,128)(2,1)} %value_w.1, bf16[896,3584]{1,0:T(8,128)(2,1)} %out_w.1, ...), custom_call_target="tpu_custom_call" | custom-call | tf_op jit(solution)/shard_map/pallas_call | solution.py:364
  66.8 0.7 %fusion = (f32[256,128]{1,0:T(8,128)}, f32[256,128]{1,0:T(8,128)}) fusion(f32[256,256]{1,0:T(8,128)S(1)} %get-tuple-element.6), kind=kLoop, calls=%fused_computation | loop fusion | bytes 524288 | tf_op jit(solution)/shard_map/slice | solution.py:409
  67.5 0.8 %copy.13 = bf16[256,896]{1,0:T(8,128)(2,1)} copy(bf16[256,896]{1,0:T(8,128)(2,1)S(1)} %get-tuple-element.12) | data formatting | bytes 917504

commit v3 on v2

v3 whole, which is shorter than its diff:
```python
import functools

import jax
import jax.numpy as jnp
from jax import lax
from jax.experimental import pallas as pl
from jax.experimental.pallas import tpu as pltpu
from jax.sharding import PartitionSpec as P

HD = 128
PBLK = 64
NX, NZ = 4, 8
TP = 4
HEADS = 7
TOK = 256
KEYS = 1024
FEAT = 896
HALF = TOK // 2
QUART = 4
QROWS = PBLK // QUART
PIECE = FEAT // (2 * NX)
SCALE = HD ** -0.5
LOG2E = 1.4426950408889634
BF = jnp.bfloat16
F32 = jnp.float32
MESH = pl.DeviceIdType.MESH
FAR_FIRST = (11, 10, 7, 15, 9, 8, 6, 14, 3, 2, 5, 13, 1, 4, 12)


def dot(a, b):
    return jnp.dot(a, b, preferred_element_type=F32)


def dot_nt(a, b):
    return lax.dot_general(a, b, (((1,), (1,)), ((), ())), preferred_element_type=F32)


def kernel(
    reads_hbm, hid, queries, key_w, value_w, out_w, pkeys, pvalues, og,
    out, grads,
    reads, hs, gs, wkv, wo, qv, qt, grp, snd, kv, vt, hot, st, es, peaks, lows, own_k, own_vt, new_own, ctxt, ctx, inv, cgacc, kvs, kvr, cgt, cgn,
    gsend, grecv, psend, precv, own_grad, rs_own, rs_fwd, rs_mid, rs_in,
    load_sem, ys_sem, yr_sem, g_send, g_recv, a_send, a_recv, b_send, b_recv, p_send, p_recv,
    r_send, r_recv, wy_send, wy_recv, wx_send, wx_recv, wc_send, wc_recv, kv_send, kv_recv,
):
    seq = lax.axis_index("seq")
    tp = lax.axis_index("tp")
    core = seq % 2
    zpos = (seq // 2) % NZ
    xpos = seq // (2 * NZ)
    member = seq % 4
    level = seq // 4
    right = (tp + 1) % TP
    left = (tp + TP - 1) % TP
    across = (tp + 2) % TP
    step = 2 * (zpos % 2) - 1

    def seq_of(x, z):
        return (x * NZ + z) * 2 + core

    def reader(r):
        i, j = r // 4, r % 4
        return seq_of((xpos + i) % NX, (zpos + step * j + NZ) % NZ)

    def server(r):
        i, j = r // 4, r % 4
        even = (zpos + j) % 2
        z = (zpos + j - 2 * j * even + NZ) % NZ
        return seq_of((xpos + NX - i) % NX, z)

    def peer(p):
        low = member
        bit0, bit1 = low % 2, low // 2
        if p % 2:
            bit0 = 1 - bit0
        if p // 2:
            bit1 = 1 - bit1
        return bit1 * 2 + bit0

    barrier = pltpu.get_barrier_semaphore()
    for t in (left, right, across):
        pl.semaphore_signal(barrier, 1, device_id={"tp": t}, device_id_type=MESH)
    for p in (1, 2, 3):
        pl.semaphore_signal(
            barrier, 1, device_id={"seq": level * 4 + peer(p)}, device_id_type=MESH
        )
    for r in range(1, 16):
        pl.semaphore_signal(barrier, 1, device_id={"seq": server(r)}, device_id_type=MESH)

    loads = []

    def load(src, dst):
        loads.append(pltpu.make_async_copy(src, dst, load_sem.at[len(loads)]))
        loads[-1].start()

    mine = grp.at[pl.ds(member * 4, 4)]
    first = [
        pltpu.make_async_copy(reads_hbm, reads, load_sem.at[9]),
        pltpu.make_async_copy(pkeys, mine.at[:, :, :, pl.ds(0, HD)], load_sem.at[10]),
        pltpu.make_async_copy(pvalues, mine.at[:, :, :, pl.ds(HD, HD)], load_sem.at[11]),
    ]
    for c in first:
        c.start()
    load(hid, hs)
    load(queries, qv)
    load(key_w.at[pl.ds(tp * FEAT, FEAT)], wkv.at[0, :, pl.ds(0, HD)])
    load(value_w.at[pl.ds(tp * FEAT, FEAT)], wkv.at[0, :, pl.ds(HD, HD)])
    load(og, gs.at[3])
    for j in range(TP):
        load(out_w.at[:, pl.ds(j * FEAT, FEAT)], wo.at[j])

    for c in first:
        c.wait()

    pl.semaphore_wait(barrier, 21)

    def ring(src, dst, k):
        lo, hi = pl.ds(0, HALF), pl.ds(HALF, HALF)

        def copy(s, d, n, to):
            return pltpu.make_async_remote_copy(
                s, d, ys_sem.at[k + n], yr_sem.at[k + n],
                device_id={"tp": to}, device_id_type=MESH,
            )

        own = [
            copy(src.at[lo], dst.at[0, lo], 0, right),
            copy(src.at[hi], dst.at[1, hi], 1, left),
            copy(src.at[hi], dst.at[0, hi], 2, right),
            copy(src.at[lo], dst.at[1, lo], 3, left),
        ]
        forward = [
            copy(dst.at[0, lo], dst.at[2, lo], 4, right),
            copy(dst.at[1, hi], dst.at[2, hi], 5, left),
        ]
        return own, forward

    piece = pl.ds((core * NX + xpos) * PIECE, PIECE)
    w_far = []
    for d in (2, 1, 3):
        to = (tp + d) % TP
        rows = pl.ds(to * FEAT + (core * NX + xpos) * PIECE, PIECE)
        for n, src in enumerate((key_w, value_w)):
            c = pltpu.make_async_remote_copy(
                src.at[rows], wkv.at[TP - d, piece, pl.ds(n * HD, HD)],
                wy_send.at[d, n], wy_recv.at[d, n], device_id={"tp": to}, device_id_type=MESH,
            )
            c.start()
            w_far.append(c)
    o_own, o_fwd = ring(og, gs, 0)
    for c in o_own:
        c.start()

    group = []
    for p in (3, 2, 1):
        c = pltpu.make_async_remote_copy(
            mine, mine,
            g_send.at[p], g_recv.at[p],
            device_id={"seq": level * 4 + peer(p)}, device_id_type=MESH,
        )
        c.start()
        group.append(c)

    rd = [lax.bitwise_and(reads[level, reader(r)], 15) for r in range(16)]
    lane = lax.broadcasted_iota(jnp.int32, (PBLK, TOK), 1)
    sub = lax.broadcasted_iota(jnp.int32, (PBLK, TOK), 0)
    want = lane % QROWS
    for r in range(16):
        want = want + jnp.where(lane // QROWS == r, rd[r] * QROWS, 0)
    for p in range(4):
        match = (sub + peer(p) * PBLK) == want
        hot[p * PBLK : (p + 1) * PBLK, :] = jnp.where(match, 1.0, 0.0).astype(BF)

    loads[1].wait()
    for h in range(HEADS):
        qt[h] = qv[:, h * HD : (h + 1) * HD].T

    for c in w_far:
        c.wait_recv()
    mate = {"seq": level * 4 + peer(1)}

    def pass_on(src_x, sems, n, to):
        rows = pl.ds((core * NX + src_x) * PIECE, PIECE)
        part = wkv.at[pl.ds(1, TP - 1), rows]
        return pltpu.make_async_remote_copy(
            part, part, sems[0].at[n], sems[1].at[n], device_id=to, device_id_type=MESH
        )

    w_row = []
    for i in (2, 1, 3):
        w_row.append(
            pass_on(xpos, (wx_send, wx_recv), i, {"seq": seq_of((xpos + i) % NX, zpos)})
        )
        w_row[-1].start()
    w_mate = [pass_on(xpos, (wc_send, wc_recv), 0, mate)]
    w_mate[0].start()

    for c in group:
        c.wait_recv()
    serve = [None]
    for q in range(QUART):
        kv[q, 0] = grp[rd[0], q]
    for r in range(1, 16):
        snd[r] = grp[rd[r]]
        c = pltpu.make_async_remote_copy(
            snd.at[r], kv.at[pl.ds(0, QUART), r], a_send.at[r], a_recv.at[r],
            device_id={"seq": reader(r)}, device_id_type=MESH,
        )
        c.start()
        serve.append(c)

    o_own[0].wait_recv()
    o_fwd[0].start()
    o_own[1].wait_recv()
    o_fwd[1].start()

    for i, c in zip((2, 1, 3), w_row):
        c.wait_recv()
        w_mate.append(pass_on((xpos + NX - i) % NX, (wc_send, wc_recv), i, mate))
        w_mate[-1].start()

    for n in range(4, 9):
        loads[n].wait()
    cgacc[...] = dot_nt(wo[tp], gs[3])
    o_own[2].wait_recv()
    cgacc[...] += dot_nt(wo[left], gs[0])
    o_own[3].wait_recv()
    cgacc[...] += dot_nt(wo[right], gs[1])

    for n in (0, 2, 3):
        loads[n].wait()
    for c in w_mate:
        c.wait_recv()
    new_far = []
    for d in (2, 1, 3):
        kvs[d] = dot(hs[...], wkv[d]).astype(BF)
        c = pltpu.make_async_remote_copy(
            kvs.at[d], kvr.at[d], kv_send.at[d], kv_recv.at[d],
            device_id={"tp": (tp + d) % TP}, device_id_type=MESH,
        )
        c.start()
        new_far.append(c)
    new_own[...] = dot(hs[...], wkv[0])

    o_fwd[0].wait_recv()
    o_fwd[1].wait_recv()
    cgacc[...] += dot_nt(wo[across], gs[2])

    for r in range(1, 16):
        serve[r].wait_recv()
    for c in range(QUART):
        vt[:, c * TOK : (c + 1) * TOK] = kv[c, :, :, HD:].reshape(TOK, HD).T

    def forward(h):
        q_h = qt[h]
        peak = None
        for c in range(QUART):
            s = dot(kv[c, :, :, 0:HD].reshape(TOK, HD), q_h)
            st[h, c] = s
            top = jnp.max(s, axis=0, keepdims=True)
            peak = top if peak is None else jnp.maximum(peak, top)
        low = None
        for c in range(QUART):
            e = jnp.exp2((st[h, c] - peak) * (SCALE * LOG2E))
            part = jnp.sum(e, axis=0, keepdims=True)
            low = part if low is None else low + part
            es[h, c * TOK : (c + 1) * TOK, :] = e.astype(BF)
        peaks[h] = jnp.broadcast_to(peak, (8, TOK))
        lows[h] = jnp.broadcast_to(low, (8, TOK))
        ctxt[h] = dot(vt[...], es[h])

    for h in range(HEADS):
        forward(h)
    for c in new_far:
        c.wait_recv()
    total = new_own[...]
    for d in (1, 2, 3):
        total += kvr[d].astype(F32)
    total = total.astype(BF)
    own_k[...] = total[:, 0:HD]
    own_vt[...] = total[:, HD:].T
    key_pos = lax.broadcasted_iota(jnp.int32, (TOK, TOK), 0)
    tok_pos = lax.broadcasted_iota(jnp.int32, (TOK, TOK), 1)
    visible = key_pos <= tok_pos
    for h in range(HEADS):
        s = jnp.where(visible, dot(own_k[...], qt[h]), -jnp.inf)
        old = peaks[h, 0:1, :]
        peak = jnp.maximum(jnp.max(s, axis=0, keepdims=True), old)
        e = jnp.exp2((s - peak) * (SCALE * LOG2E))
        shrink = jnp.exp2((old - peak) * (SCALE * LOG2E))
        low = lows[h, 0:1, :] * shrink + jnp.sum(e, axis=0, keepdims=True)
        scale = 1.0 / low
        gain = shrink * scale
        inv[h] = jnp.broadcast_to(gain, (8, TOK))
        joined = ctxt[h] * gain + dot(own_vt[...], e.astype(BF)) * scale
        ctxt[h] = joined
        ctx[:, h * HD : (h + 1) * HD] = joined.astype(BF).T

    def rs(src, dst, n, to):
        return pltpu.make_async_remote_copy(
            src, dst, r_send.at[n], r_recv.at[n], device_id={"tp": to}, device_id_type=MESH
        )

    lo, hi = pl.ds(0, HALF), pl.ds(HALF, HALF)
    rs_far = [
        rs(rs_fwd.at[lo], rs_mid.at[0], 0, right),
        rs(rs_fwd.at[hi], rs_mid.at[1], 1, left),
    ]
    rs_now = [
        rs(rs_own.at[0, hi], rs_in.at[0, hi], 2, right),
        rs(rs_own.at[1, lo], rs_in.at[1, lo], 3, left),
    ]
    rs_late = [
        rs(rs_own.at[0, lo], rs_in.at[0, lo], 4, right),
        rs(rs_own.at[1, hi], rs_in.at[1, hi], 5, left),
    ]
    rs_fwd[...] = dot(ctx[...], wo[across]).astype(BF)
    for c in rs_far:
        c.start()
    for h in range(HEADS):
        scaled = (cgacc[h * HD : (h + 1) * HD, :] * inv[h, 0:1, :]).astype(BF)
        cgt[h] = scaled
        cgn[h] = scaled.T
        delta = jnp.sum(scaled.astype(F32) * ctxt[h], axis=0, keepdims=True)
        inv[h] = jnp.broadcast_to(delta, (8, TOK))

    back = []

    def backward(i):
        rows = slice(i * TOK, (i + 1) * TOK)
        vals = kv[i, :, :, HD:].reshape(TOK, HD)
        dk = None
        for h in range(HEADS):
            slope = dot(vals, cgt[h])
            e = es[h, rows, :]
            grad = (e.astype(F32) * (slope - inv[h, 0:1, :])).astype(BF)
            dk_h = dot(grad, qv[:, h * HD : (h + 1) * HD])
            dv_h = dot(e, cgn[h])
            dk = dk_h if dk is None else dk + dk_h
            dv = dv_h if h == 0 else dv + dv_h
        gsend[i, :, :, 0:HD] = dk.astype(BF).reshape(16, QROWS, HD)
        gsend[i, :, :, HD:] = dv.astype(BF).reshape(16, QROWS, HD)
        grecv[i, 0] = gsend[i, 0]
        copies = []
        for r in FAR_FIRST:
            c = pltpu.make_async_remote_copy(
                gsend.at[i, r], grecv.at[i, r], b_send.at[i, r], b_recv.at[i, r],
                device_id={"seq": server(r)}, device_id_type=MESH,
            )
            c.start()
            copies.append(c)
        back.append(copies)

    backward(0)
    rs_own[0] = dot(ctx[...], wo[right]).astype(BF)
    rs_own[1] = dot(ctx[...], wo[left]).astype(BF)
    for c in rs_now:
        c.start()
    backward(1)
    rs_far[0].wait_recv()
    rs_own[0, 0:HALF] = (rs_own[0, 0:HALF].astype(F32) + rs_mid[0].astype(F32)).astype(BF)
    rs_late[0].start()
    rs_far[1].wait_recv()
    rs_own[1, HALF:] = (rs_own[1, HALF:].astype(F32) + rs_mid[1].astype(F32)).astype(BF)
    rs_late[1].start()
    backward(2)
    backward(3)

    kept = dot(ctx[...], wo[tp])

    spread = []
    for i in range(QUART):
        for c in back[i]:
            c.wait_recv()
        part = dot(hot[...], grecv[i].reshape(TOK, 2 * HD))
        own_grad[i] = part[0:PBLK, :]
        for p in (3, 2, 1):
            psend[p, i] = part[p * PBLK : (p + 1) * PBLK, :].astype(BF)
            c = pltpu.make_async_remote_copy(
                psend.at[p, i], precv.at[p, i], p_send.at[p, i], p_recv.at[p, i],
                device_id={"seq": level * 4 + peer(p)}, device_id_type=MESH,
            )
            c.start()
            spread.append(c)

    for c in rs_now + rs_late:
        c.wait_recv()
    out[...] = (kept + rs_in[0].astype(F32) + rs_in[1].astype(F32)).astype(BF)

    for i in range(QUART):
        for c in spread[3 * i : 3 * i + 3]:
            c.wait_recv()
        total = own_grad[i]
        for p in (1, 2, 3):
            total = total + precv[p, i].astype(F32)
        grads[:, i, :, 0:HD] = (total[:, 0:HD] * SCALE).reshape(4, QROWS, HD)
        grads[:, i, :, HD:] = total[:, HD:].reshape(4, QROWS, HD)

    for c in w_far + w_row + w_mate + new_far + o_own + o_fwd + group + rs_far + rs_now + rs_late + spread:
        c.wait_send()
    for r in range(1, 16):
        serve[r].wait_send()
    for copies in back:
        for c in copies:
            c.wait_send()


def local(*args):
    hidden, queries, key_w, value_w, out_w, pkeys, pvalues, reads, og = args
    pkeys = pkeys.reshape(4, QUART, QROWS, HD)
    pvalues = pvalues.reshape(4, QUART, QROWS, HD)
    operands = (reads.T, hidden, queries, key_w, value_w, out_w, pkeys, pvalues, og)
    operands = [pltpu.with_memory_space_constraint(a, pltpu.HBM) for a in operands]
    vmem = pl.BlockSpec(memory_space=pltpu.VMEM)
    hbm = pl.BlockSpec(memory_space=pltpu.HBM)
    dma = pltpu.SemaphoreType.DMA
    V = pltpu.VMEM
    out, grads = pl.pallas_call(
        kernel,
        out_shape=(
            jax.ShapeDtypeStruct((TOK, FEAT), BF),
            jax.ShapeDtypeStruct((4, QUART, QROWS, 2 * HD), F32),
        ),
        in_specs=[hbm] * 9,
        out_specs=(vmem, vmem),
        scratch_shapes=[
            pltpu.SMEM((16, 64), jnp.int32),
            V((TOK, FEAT), BF),
            V((4, TOK, FEAT), BF),
            V((TP, FEAT, 2 * HD), BF),
            V((TP, FEAT, FEAT), BF),
            V((TOK, FEAT), BF),
            V((HEADS, HD, TOK), BF),
            V((16, QUART, QROWS, 2 * HD), BF),
            V((16, QUART, QROWS, 2 * HD), BF),
            V((QUART, 16, QROWS, 2 * HD), BF),
            V((HD, KEYS), BF),
            V((TOK, TOK), BF),
            V((HEADS, QUART, TOK, TOK), F32),
            V((HEADS, KEYS, TOK), BF),
            V((HEADS, 8, TOK), F32),
            V((HEADS, 8, TOK), F32),
            V((TOK, HD), BF),
            V((HD, TOK), BF),
            V((TOK, 2 * HD), F32),
            V((HEADS, HD, TOK), F32),
            V((TOK, FEAT), BF),
            V((HEADS, 8, TOK), F32),
            V((FEAT, TOK), F32),
            V((TP, TOK, 2 * HD), BF),
            V((TP, TOK, 2 * HD), BF),
            V((HEADS, HD, TOK), BF),
            V((HEADS, TOK, HD), BF),
            V((QUART, 16, QROWS, 2 * HD), BF),
            V((QUART, 16, QROWS, 2 * HD), BF),
            V((4, QUART, PBLK, 2 * HD), BF),
            V((4, QUART, PBLK, 2 * HD), BF),
            V((QUART, PBLK, 2 * HD), F32),
            V((2, TOK, FEAT), BF),
            V((TOK, FEAT), BF),
            V((2, HALF, FEAT), BF),
            V((2, TOK, FEAT), BF),
            dma((12,)), dma((6,)), dma((6,)), dma((4,)), dma((4,)), dma((16,)), dma((16,)),
            dma((QUART, 16)), dma((QUART, 16)), dma((4, QUART)), dma((4, QUART)), dma((6,)), dma((6,)),
            dma((4, 2)), dma((4, 2)), dma((4,)), dma((4,)), dma((4,)), dma((4,)), dma((4,)), dma((4,)),
        ],
        compiler_params=pltpu.CompilerParams(
            collective_id=0, has_side_effects=True, vmem_limit_bytes=40 * 1024 * 1024
        ),
    )(*operands)
    grads = grads.reshape(TOK, 2 * HD)
    return out, grads[:, 0:HD], grads[:, HD:]


def solution(mesh):
    in_specs = (
        P("seq", "tp"), P("seq", "tp"), P(None, "tp"), P(None, "tp"), P("tp", None),
        P("seq", "tp"), P("seq", "tp"), P(), P("seq", "tp"),
    )
    out_specs = (P("seq", "tp"), P("seq", "tp"), P("seq", "tp"))
    return jax.shard_map(local, mesh=mesh, in_specs=in_specs, out_specs=out_specs, check_vma=False)
```

time: 68.4 us -> 65.7 us (0.961)
  Pallas kernels: 66.2 us -> 63.4 us
    pallas_call x1, Pallas kernels: 66.2 us -> 63.4 us  [local(): pl.pallas_call(kernel, out_shape=(jax.ShapeDtypeStruct((TOK, FEAT), BF),...]
where the time goes in v3:
time: 65.7 us; the launch traced here: 65.5 us
  Pallas kernels  63.4 us (96%)
  local copies, waits for them, and re-layouts  1.48 us (2%)
    pallas_call x1, Pallas kernels, local(): pl.pallas_call(kernel, out_shape=(jax.ShapeDtypeStruct((TOK, FEAT), BF),...  63.4 us

profile of v3, /device:TPU:1, one launch (start us, length us, event | category | flops | bytes accessed | tf_op | source)
XLA Modules:
  0.0 65.5 jit_solution(17187225056284011947)
XLA Ops:
  0.6 63.4 %shard_map.112 = (bf16[256,896]{1,0:T(8,128)(2,1)S(1)}, f32[4,4,16,256]{3,2,1,0:T(8,128)S(1)}) custom-call(s32[16,64]{1,0:T(8,128)} %bitcast.7, bf16[256,896]{1,0:T(8,128)(2,1)} %hid.1, bf16[256,896]{1,0:T(8,128)(2,1)} %queries.1, bf16[3584,128]{1,0:T(8,128)(2,1)} %key_w.1, bf16[3584,128]{1,0:T(8,128)(2,1)} %value_w.1, bf16[896,3584]{1,0:T(8,128)(2,1)} %out_w.1, ...), custom_call_target="tpu_custom_call" | custom-call | tf_op jit(solution)/shard_map/pallas_call | solution.py:418
  64.0 0.7 %fusion = (f32[256,128]{1,0:T(8,128)}, f32[256,128]{1,0:T(8,128)}) fusion(f32[256,256]{1,0:T(8,128)S(1)} %bitcast.4), kind=kLoop, calls=%fused_computation | loop fusion | bytes 524288 | tf_op jit(solution)/shard_map/slice | solution.py:472
  64.7 0.8 %copy.13 = bf16[256,896]{1,0:T(8,128)(2,1)} copy(bf16[256,896]{1,0:T(8,128)(2,1)S(1)} %get-tuple-element.12) | data formatting | bytes 917504

commit v4 on v3

--- a/solution.py
+++ b/solution.py
@@ -38,7 +38,7 @@
 def kernel(
     reads_hbm, hid, queries, key_w, value_w, out_w, pkeys, pvalues, og,
     out, grads,
-    reads, hs, gs, wkv, wo, qv, qt, grp, snd, kv, vt, hot, st, es, peaks, lows, own_k, own_vt, new_own, ctxt, ctx, inv, cgacc, kvs, kvr, cgt, cgn,
+    reads, hs, gs, wkv, wo, qv, qt, grp, snd, kv, vt, hot, st, es, peaks, lows, own_k, own_vt, new_own, ctxt, ctx, inv, cgacc, kvs, kvr, cgt,
     gsend, grecv, psend, precv, own_grad, rs_own, rs_fwd, rs_mid, rs_in,
     load_sem, ys_sem, yr_sem, g_send, g_recv, a_send, a_recv, b_send, b_recv, p_send, p_recv,
     r_send, r_recv, wy_send, wy_recv, wx_send, wx_recv, wc_send, wc_recv, kv_send, kv_recv,
@@ -320,7 +320,6 @@
     for h in range(HEADS):
         scaled = (cgacc[h * HD : (h + 1) * HD, :] * inv[h, 0:1, :]).astype(BF)
         cgt[h] = scaled
-        cgn[h] = scaled.T
         delta = jnp.sum(scaled.astype(F32) * ctxt[h], axis=0, keepdims=True)
         inv[h] = jnp.broadcast_to(delta, (8, TOK))
 
@@ -335,7 +334,7 @@
             e = es[h, rows, :]
             grad = (e.astype(F32) * (slope - inv[h, 0:1, :])).astype(BF)
             dk_h = dot(grad, qv[:, h * HD : (h + 1) * HD])
-            dv_h = dot(e, cgn[h])
+            dv_h = dot_nt(e, cgt[h])
             dk = dk_h if dk is None else dk + dk_h
             dv = dv_h if h == 0 else dv + dv_h
         gsend[i, :, :, 0:HD] = dk.astype(BF).reshape(16, QROWS, HD)
@@ -450,7 +449,6 @@
             V((TP, TOK, 2 * HD), BF),
             V((TP, TOK, 2 * HD), BF),
             V((HEADS, HD, TOK), BF),
-            V((HEADS, TOK, HD), BF),
             V((QUART, 16, QROWS, 2 * HD), BF),
             V((QUART, 16, QROWS, 2 * HD), BF),
             V((4, QUART, PBLK, 2 * HD), BF),

time: 65.7 us -> 65.7 us (level)
  no operation moved by 1% of the time
where the time goes in v4:
time: 65.7 us; the launch traced here: 65.3 us
  Pallas kernels  63.2 us (96%)
  local copies, waits for them, and re-layouts  1.48 us (2%)
    pallas_call x1, Pallas kernels, local(): pl.pallas_call(kernel, out_shape=(jax.ShapeDtypeStruct((TOK, FEAT), BF),...  63.2 us

profile of v4, /device:TPU:1, one launch (start us, length us, event | category | flops | bytes accessed | tf_op | source)
XLA Modules:
  0.0 65.3 jit_solution(6731333674005494888)
XLA Ops:
  0.6 63.2 %shard_map.112 = (bf16[256,896]{1,0:T(8,128)(2,1)S(1)}, f32[4,4,16,256]{3,2,1,0:T(8,128)S(1)}) custom-call(s32[16,64]{1,0:T(8,128)} %bitcast.7, bf16[256,896]{1,0:T(8,128)(2,1)} %hid.1, bf16[256,896]{1,0:T(8,128)(2,1)} %queries.1, bf16[3584,128]{1,0:T(8,128)(2,1)} %key_w.1, bf16[3584,128]{1,0:T(8,128)(2,1)} %value_w.1, bf16[896,3584]{1,0:T(8,128)(2,1)} %out_w.1, ...), custom_call_target="tpu_custom_call" | custom-call | tf_op jit(solution)/shard_map/pallas_call | solution.py:417
  63.8 0.7 %fusion = (f32[256,128]{1,0:T(8,128)}, f32[256,128]{1,0:T(8,128)}) fusion(f32[256,256]{1,0:T(8,128)S(1)} %bitcast.4), kind=kLoop, calls=%fused_computation | loop fusion | bytes 524288 | tf_op jit(solution)/shard_map/slice | solution.py:470
  64.5 0.8 %copy.13 = bf16[256,896]{1,0:T(8,128)(2,1)} copy(bf16[256,896]{1,0:T(8,128)(2,1)S(1)} %get-tuple-element.12) | data formatting | bytes 917504
